TPU v7x, 32 devices: a whole 2x2x4 slice. The times are simulated.
32 devices in a mesh: snap: 2 (over x), row: 16 (over z, y, core).
Axes of the slice: x: 2, y: 2, z: 4, core: 2. Of those that a mesh axis runs over, the one named last changes fastest.
Arguments:
- snapshots: bfloat16 [256, 262144], P('snap', 'row'), may hold values from -64 to 64
- counts: int32 [16], P('row'), may hold values from 1 to 16384, 196608 in all
Outputs:
- basis: bfloat16 [256, 262144], P('snap', 'row')
- r_factor: float32 [256, 256], replicated
Inputs may be any that keep to these rules, and one draw needn't show every extreme that they name: `counts`: at least one row and at most 16384 rows are live on each index of row, and some index has all 16384 live.
All inputs are finite; a program needn't handle non-finite values. No bound on the sum of `counts` on one device may be relied on, other than what follows from the above.
Results may differ from a plain program's by a relative error of at most 0.0049.
Values may be sent and summed in bfloat16 or wider, within the bound.
A program may use at most 64 MiB of HBM per device.

v0:
```python
import math
import jax
import jax.numpy as jnp
from jax import lax
from jax.sharding import PartitionSpec as P


def gram_of(block):
    return lax.dot_general(
        block, block, (((1,), (1,)), ((), ())), preferred_element_type=jnp.float32
    )


def factors(gram, scale):
    lower = jnp.linalg.cholesky(gram)
    r_factor = lower.T / scale
    width = gram.shape[0]
    inverse = lax.linalg.triangular_solve(
        lower, jnp.eye(width, dtype=jnp.float32), left_side=True, lower=True
    ).T
    weights = (inverse * scale).astype(jnp.bfloat16)
    return (r_factor, weights)


def apply_weights(weights, block):
    return lax.dot_general(
        weights, block, (((0,), (0,)), ((), ())), preferred_element_type=jnp.float32
    ).astype(jnp.bfloat16)


def shards(snapshots, counts):
    narrow, slots = snapshots.shape
    slot = lax.broadcasted_iota(jnp.int32, (1, slots), 1)
    live = jnp.where(slot < counts[0], snapshots, jnp.zeros_like(snapshots))
    scale = math.sqrt(slots * lax.axis_size("row"))
    whole = lax.all_gather(live, "snap", axis=0, tiled=True)
    gram = lax.psum(gram_of(whole), "row")
    r_factor, weights = factors(gram, scale)
    start = lax.axis_index("snap") * narrow
    own_weights = lax.dynamic_slice_in_dim(weights, start, narrow, 1)
    basis = apply_weights(own_weights, whole)
    return (basis, r_factor)


def solution(mesh):
    placed = (P("snap", "row"), P("row"))
    return jax.shard_map(
        shards, mesh=mesh, in_specs=placed, out_specs=(P("snap", "row"), P()), check_vma=False
    )
```

profile of v0, /device:TPU:0, one launch (start us, length us, event | category | flops | bytes accessed | tf_op | source)
XLA Modules:
  0.0 294.9 jit_solution(8530265544125170200)
XLA Ops:
  7.2 0.0 all-gather.2.cloned.1.call-start
  7.9 4.8 %broadcast_select_fusion = bf16[128,16384]{1,0:T(8,128)(2,1)} fusion(bf16[128,16384]{1,0:T(8,128)(2,1)} %param.2, pred[16384]{0:T(1024)(128)(4,1)S(1)} %iota_compare_fusion.3), kind=kLoop, calls=%fused_computation.3 | loop fusion | flops 2097152 | bytes 8404992 | tf_op jit(solution)/shard_map/jit(_where)/select_n | solution.py:34
  12.7 0.0 all-gather.2.cloned.1.call-update
  12.7 0.0 all-reduce.3.cloned.1.call-start
  12.7 106.8 %all-gather.2.cloned.1.call-done = bf16[256,16384]{1,0:T(8,128)(2,1)} async-done(((bf16[128,16384]{1,0:T(8,128)(2,1)}), bf16[256,16384]{1,0:T(8,128)(2,1)}) %all-gather.2.cloned.1.call-update) | async-done | bytes 8388624 | tf_op jit(solution)/shard_map/all_gather | solution.py:36
  119.5 8.8 %fusion.18 = f32[256,256]{0,1:T(8,128)} fusion(bf16[256,16384]{1,0:T(8,128)(2,1)} %all-gather.2.cloned.1.call-done), kind=kOutput, calls=%fused_computation.43 | convolution fusion | flops 2147483648 | bytes 8650752 | tf_op jit(solution)/shard_map/dot_general | solution.py:9
  128.4 0.0 all-reduce.3.cloned.1.call-update
  128.5 89.8 %all-reduce.3.cloned.1.call-done = f32[256,256]{0,1:T(8,128)} async-done(((f32[256,256]{0,1:T(8,128)}), f32[256,256]{0,1:T(8,128)}) %all-reduce.3.cloned.1.call-update) | async-done | bytes 262160 | tf_op jit(solution)/shard_map/psum | solution.py:37
  218.2 1.1 copy.5
  219.3 1.0 fusion
  220.3 11.7 %cholesky.50 = f32[128,128]{1,0:T(8,128)S(1)} custom-call(f32[128,128]{1,0:T(8,128)S(1)} %cholesky.118), custom_call_target="Cholesky" | custom-call | tf_op jit(solution)/shard_map/jit(cholesky)/cholesky | solution.py:15
  232.1 9.8 %custom-call.14 = f32[1,128,128]{1,2,0:T(8,128)S(1)} custom-call(f32[1,128,128]{2,1,0:T(8,128)S(1)} %get-tuple-element.27), custom_call_target="InvertDiagBlocksLowerTriangular" | custom-call | tf_op jit(solution)/shard_map/jit(cholesky)/cholesky | solution.py:15
  241.9 0.2 constant_dynamic-update-slice_fusion
  242.1 0.3 convolution_subtract_fusion.1
  242.4 11.8 %cholesky.105 = f32[128,128]{1,0:T(8,128)S(1)} custom-call(f32[128,128]{1,0:T(8,128)S(1)} %convolution_subtract_fusion.1), custom_call_target="Cholesky" | custom-call | tf_op jit(solution)/shard_map/jit(cholesky)/cholesky | solution.py:15
  254.3 0.6 compare_reduce_fusion
  256.2 0.8 copy.6
  257.0 0.1 triangular_solve.63
  257.1 3.7 %while.1 = (s32[]{:T(128)}, f32[256,256]{1,0:T(8,128)S(1)}, s32[2,2]{1,0:T(2,128)S(1)}, f32[2,128,128]{2,1,0:T(8,128)S(1)}, s32[]{:T(128)}) while((s32[]{:T(128)}, f32[256,256]{1,0:T(8,128)S(1)}, s32[2,2]{1,0:T(2,128)S(1)}, f32[2,128,128]{2,1,0:T(8,128)S(1)}, s32[]{:T(128)}) %tuple.29), condition=%wide.while_cond, body=%wide.while_body.sunk | while | flops 2 | bytes 131189 | solution.py:18
  257.1 0.6 fusion.27
  257.6 1.3 bitcast_dynamic-update-slice_fusion.2
  259.0 0.6 fusion.27
  259.5 1.3 bitcast_dynamic-update-slice_fusion.2
  260.8 19.7 %custom-call.15 = f32[2,128,128]{1,2,0:T(8,128)S(1)} custom-call(f32[2,128,128]{2,1,0:T(8,128)S(1)} %get-tuple-element.9), custom_call_target="InvertDiagBlocksLowerTriangular" | custom-call | tf_op jit(solution)/shard_map/triangular_solve | solution.py:18
  280.5 0.3 fusion.5
  280.8 0.3 convolution_subtract_fusion
  281.0 0.3 fusion.10
  281.4 6.7 %convolution_convert_fusion = bf16[128,16384]{1,0:T(8,128)(2,1)} fusion(bf16[256,16384]{1,0:T(8,128)(2,1)} %all-gather.2.cloned.1.call-done, s32[]{:T(128)S(6)} %select_n.13, f32[128,256]{1,0:T(8,128)S(1)} %fusion.5, f32[128,256]{1,0:T(8,128)S(1)} %fusion.10), kind=kOutput, calls=%fused_computation.2 | convolution fusion | flops 1075937280 | bytes 12845060 | tf_op jit(solution)/shard_map/dot_general | solution.py:26
  (11 shorter events, 0.2 us)
Async XLA Ops:
  7.2 112.4 %all-gather.2.cloned.1.call-start = ((), (), s32[]{:S(2)}) async-start(), calls=%async_computation | async-start | bytes 12582912 | tf_op jit(solution)/shard_map/all_gather | solution.py:36
  12.7 205.6 %all-reduce.3.cloned.1.call-start = ((), (), s32[]{:S(2)}) async-start(), calls=%async_computation.1 | async-start | bytes 524288 | tf_op jit(solution)/shard_map/psum | solution.py:37
Sparse Core Ops, SparseCore 0:
  12.8 106.6 all-gather.1
  128.5 89.6 all-reduce.2
where the time goes:
time: 295 us
  waiting for transfers between devices  197 us (67%)
  other arithmetic  59.6 us (20%)
  matrix products  16.8 us (6%)
  between operations  16 us (5%)
  local copies, waits for them, and re-layouts  5.71 us (2%)
    all_gather x1, waiting for transfers between devices, shards(): whole = lax.all_gather(live, 'snap', axis=0, tiled=True)  107 us
    psum x1, waiting for transfers between devices, shards(): gram = lax.psum(gram_of(whole), 'row')  89.8 us
    another operation x6, other arithmetic, factors(): lower = jnp.linalg.cholesky(gram)  34.1 us
    another operation x2, other arithmetic, factors(): lax.linalg.triangular_solve(lower, jnp.eye(width, dtype=jnp.float32), lef...  19.7 us
    dot_general x1, matrix products, gram_of(): lax.dot_general(block, block, (((1,), (1,)), ((), ())), preferred_element...  8.83 us
    dot_general x1, matrix products, apply_weights(): lax.dot_general(weights, block, (((0,), (0,)), ((), ())), preferred_eleme...  6.7 us
  transfers between devices with their start and end apart: 2, of which 2 were waited for; matrix products, arithmetic and copies ran while one was open for 0% of the time, Pallas kernels for 0%

commit v1 on v0

--- a/solution.py
+++ b/solution.py
@@ -34,7 +34,7 @@
     live = jnp.where(slot < counts[0], snapshots, jnp.zeros_like(snapshots))
     scale = math.sqrt(slots * lax.axis_size("row"))
     whole = lax.all_gather(live, "snap", axis=0, tiled=True)
-    gram = lax.psum(gram_of(whole), "row")
+    gram = jnp.sum(lax.all_gather(gram_of(whole), "row"), axis=0)
     r_factor, weights = factors(gram, scale)
     start = lax.axis_index("snap") * narrow
     own_weights = lax.dynamic_slice_in_dim(weights, start, narrow, 1)

time: 295 us -> 256 us (0.87)
  waiting for transfers between devices: 197 us -> 157 us
    psum x1 -> x0, waiting for transfers between devices: 89.8 us -> none  [shards(): gram = lax.psum(gram_of(whole), 'row')]
    all_gather x0 -> x1, waiting for transfers between devices: none -> 50.5 us  [shards(): gram = jnp.sum(lax.all_gather(gram_of(whole), 'row'), axis=0)]
where the time goes in v1:
time: 256 us
  waiting for transfers between devices  157 us (61%)
  other arithmetic  61.2 us (24%)
  matrix products  16.8 us (7%)
  between operations  16 us (6%)
  local copies, waits for them, and re-layouts  4.76 us (2%)
    all_gather x1, waiting for transfers between devices, shards(): whole = lax.all_gather(live, 'snap', axis=0, tiled=True)  107 us
    all_gather x1, waiting for transfers between devices, shards(): gram = jnp.sum(lax.all_gather(gram_of(whole), 'row'), axis=0)  50.5 us
    another operation x6, other arithmetic, factors(): lower = jnp.linalg.cholesky(gram)  34.1 us
    another operation x2, other arithmetic, factors(): lax.linalg.triangular_solve(lower, jnp.eye(width, dtype=jnp.float32), lef...  19.7 us
    dot_general x1, matrix products, gram_of(): lax.dot_general(block, block, (((1,), (1,)), ((), ())), preferred_element...  8.83 us
    dot_general x1, matrix products, apply_weights(): lax.dot_general(weights, block, (((0,), (0,)), ((), ())), preferred_eleme...  6.7 us
  transfers between devices with their start and end apart: 2, of which 2 were waited for; matrix products, arithmetic and copies ran while one was open for 0% of the time, Pallas kernels for 0%

profile of v1, /device:TPU:0, one launch (start us, length us, event | category | flops | bytes accessed | tf_op | source)
XLA Modules:
  0.0 256.2 jit_solution(17491763548164672331)
XLA Ops:
  7.2 0.0 all-gather.4.cloned.1.call-start
  7.9 4.8 %broadcast_select_fusion = bf16[128,16384]{1,0:T(8,128)(2,1)} fusion(bf16[128,16384]{1,0:T(8,128)(2,1)} %param.2, pred[16384]{0:T(1024)(128)(4,1)S(1)} %iota_compare_fusion.3), kind=kLoop, calls=%fused_computation.3 | loop fusion | flops 2097152 | bytes 8404992 | tf_op jit(solution)/shard_map/jit(_where)/select_n | solution.py:34
  12.7 0.0 all-gather.4.cloned.1.call-update
  12.7 0.0 all-gather.6.cloned.1.call-start
  12.7 106.8 %all-gather.4.cloned.1.call-done = bf16[256,16384]{1,0:T(8,128)(2,1)} async-done(((bf16[128,16384]{1,0:T(8,128)(2,1)}), bf16[256,16384]{1,0:T(8,128)(2,1)}) %all-gather.4.cloned.1.call-update) | async-done | bytes 8388624 | tf_op jit(solution)/shard_map/all_gather | solution.py:36
  119.5 8.8 %fusion.18 = f32[256,256]{1,0:T(8,128)} fusion(bf16[256,16384]{1,0:T(8,128)(2,1)} %all-gather.4.cloned.1.call-done), kind=kOutput, calls=%fused_computation.43 | convolution fusion | flops 2147483648 | bytes 8650752 | tf_op jit(solution)/shard_map/dot_general | solution.py:9
  128.4 0.0 all-gather.6.cloned.1.call-update
  128.5 50.5 %all-gather.6.cloned.1.call-done = f32[4096,256]{1,0:T(8,128)} async-done(((f32[256,256]{1,0:T(8,128)}), f32[4096,256]{1,0:T(8,128)}) %all-gather.6.cloned.1.call-update) | async-done | bytes 4194320 | tf_op jit(solution)/shard_map/all_gather | solution.py:37
  178.9 2.5 reduce_sum.9
  181.4 0.1 copy.6
  181.6 11.7 %cholesky.50 = f32[128,128]{1,0:T(8,128)S(1)} custom-call(f32[128,128]{1,0:T(8,128)S(1)} %cholesky.118), custom_call_target="Cholesky" | custom-call | tf_op jit(solution)/shard_map/jit(cholesky)/cholesky | solution.py:15
  193.4 9.8 %custom-call.14 = f32[1,128,128]{1,2,0:T(8,128)S(1)} custom-call(f32[1,128,128]{2,1,0:T(8,128)S(1)} %get-tuple-element.29), custom_call_target="InvertDiagBlocksLowerTriangular" | custom-call | tf_op jit(solution)/shard_map/jit(cholesky)/cholesky | solution.py:15
  203.2 0.2 constant_dynamic-update-slice_fusion
  203.4 0.3 convolution_subtract_fusion.1
  203.7 11.9 %cholesky.105 = f32[128,128]{1,0:T(8,128)S(1)} custom-call(f32[128,128]{1,0:T(8,128)S(1)} %convolution_subtract_fusion.1), custom_call_target="Cholesky" | custom-call | tf_op jit(solution)/shard_map/jit(cholesky)/cholesky | solution.py:15
  215.6 0.6 compare_reduce_fusion
  217.5 0.8 copy.7
  218.3 0.1 triangular_solve.63
  218.4 3.7 %while.1 = (s32[]{:T(128)}, f32[256,256]{1,0:T(8,128)S(1)}, s32[2,2]{1,0:T(2,128)S(1)}, f32[2,128,128]{2,1,0:T(8,128)S(1)}, s32[]{:T(128)}) while((s32[]{:T(128)}, f32[256,256]{1,0:T(8,128)S(1)}, s32[2,2]{1,0:T(2,128)S(1)}, f32[2,128,128]{2,1,0:T(8,128)S(1)}, s32[]{:T(128)}) %tuple.30), condition=%wide.while_cond, body=%wide.while_body.sunk | while | flops 2 | bytes 131189 | solution.py:18
  218.4 0.6 fusion.27
  219.0 1.3 bitcast_dynamic-update-slice_fusion.2
  220.3 0.6 fusion.27
  220.8 1.3 bitcast_dynamic-update-slice_fusion.2
  222.1 19.7 %custom-call.15 = f32[2,128,128]{1,2,0:T(8,128)S(1)} custom-call(f32[2,128,128]{2,1,0:T(8,128)S(1)} %get-tuple-element.9), custom_call_target="InvertDiagBlocksLowerTriangular" | custom-call | tf_op jit(solution)/shard_map/triangular_solve | solution.py:18
  241.8 0.3 fusion.5
  242.1 0.3 convolution_subtract_fusion
  242.4 0.3 fusion.10
  242.7 6.7 %convolution_convert_fusion = bf16[128,16384]{1,0:T(8,128)(2,1)} fusion(bf16[256,16384]{1,0:T(8,128)(2,1)} %all-gather.4.cloned.1.call-done, s32[]{:T(128)S(6)} %select_n.13, f32[128,256]{1,0:T(8,128)S(1)} %fusion.5, f32[128,256]{1,0:T(8,128)S(1)} %fusion.10), kind=kOutput, calls=%fused_computation.2 | convolution fusion | flops 1075937280 | bytes 12845060 | tf_op jit(solution)/shard_map/dot_general | solution.py:26
  (12 shorter events, 0.2 us)
Async XLA Ops:
  7.2 112.4 %all-gather.4.cloned.1.call-start = ((), (), s32[]{:S(2)}) async-start(), calls=%async_computation | async-start | bytes 12582912 | tf_op jit(solution)/shard_map/all_gather | solution.py:36
  12.7 166.2 %all-gather.6.cloned.1.call-start = ((), (), s32[]{:S(2)}) async-start(), calls=%async_computation.1 | async-start | bytes 4456448 | tf_op jit(solution)/shard_map/all_gather | solution.py:37
Sparse Core Ops, SparseCore 0:
  12.8 106.6 all-gather.3
  128.5 50.3 all-gather.5
